TPU v7x, 512 devices: a whole 4x8x8 slice. The times are simulated.
512 devices in a mesh: dp: 32 (over y_lo, z), mp: 16 (over x, y_hi, core).
Axes of the slice: x: 4, y: 8 (y_hi: 2, y_lo: 4; y = y_hi * 4 + y_lo), z: 8, core: 2. Of those that a mesh axis runs over, the one named last changes fastest.
Arguments:
- queries: bfloat16 [4096, 4096], P('dp', 'mp'), may hold values from -64 to 64
- database: bfloat16 [16384, 896], P('dp'), may hold values from -9 to 9
- key_weight: bfloat16 [896, 4096], P(None, 'mp'), may hold values from -1 to 2
- value_weight: bfloat16 [896, 4096], P(None, 'mp'), may hold values from -0.1875 to 0.1875
- out_weight: bfloat16 [4096, 8192], P('mp', 'dp'), may hold values from -0.1875 to 0.1875
- neighbours: int32 [64, 2], P('dp'), may hold values from 0 to 127, as said below
Outputs:
- mixed: bfloat16 [4096, 8192], P('dp', 'mp')
Inputs may be any that keep to these rules, and one draw needn't show every extreme that they name: neighbours[c, n] names block neighbours[c, n] % 4 of database shard neighbours[c, n] // 4; among the 4 neighbours of the spans 2 * i to 2 * i + 1, no two lie in the same shard.
All inputs are finite; a program needn't handle non-finite values.
Results may differ from a plain program's by a relative error of at most 0.018.
Values may be sent and summed in bfloat16 or wider, within the bound.
No kernel may reach another device: no remote copies, remote signals or barrier semaphores. Data moves between devices by JAX's collectives and lax.ppermute only.
A program may use at most 64 MiB of HBM per device.

v0:
```python
import math
import jax
import jax.numpy as jnp
from jax import lax
from jax.sharding import PartitionSpec as P

HEAD_DIM = 128
SPAN = 64
NEIGH = 2
NROW = 128
BLK_DEV = 4


def on_device(queries, database, key_weight, value_weight, out_weight, neighbours):
    shard_count = lax.axis_size("dp")
    span_count = neighbours.shape[0]
    inner_width = key_weight.shape[1]
    enc_width = database.shape[1]
    head_count = inner_width // HEAD_DIM
    flat_ids = neighbours.reshape(-1)
    shard_of = flat_ids // BLK_DEV
    local_of = flat_ids % BLK_DEV
    matches = shard_of[None, :] == jnp.arange(shard_count, dtype=jnp.int32)[:, None]
    wanted = jnp.sum(jnp.where(matches, local_of[None, :], 0), axis=1).reshape(shard_count, 1)
    requested = lax.all_to_all(wanted, "dp", split_axis=0, concat_axis=0, tiled=True)
    stored = database.reshape(BLK_DEV, NROW, enc_width)
    outgoing = stored[requested[:, 0]]
    arrived = lax.all_to_all(outgoing, "dp", split_axis=0, concat_axis=0, tiled=True)
    encoded_rows = arrived[shard_of].reshape(-1, enc_width)
    near_keys = jnp.dot(encoded_rows, key_weight, preferred_element_type=jnp.float32).astype(
        jnp.bfloat16
    )
    near_values = jnp.dot(encoded_rows, value_weight, preferred_element_type=jnp.float32).astype(
        jnp.bfloat16
    )
    key_blocks = near_keys.reshape(span_count, NEIGH * NROW, head_count, HEAD_DIM)
    value_blocks = near_values.reshape(span_count, NEIGH * NROW, head_count, HEAD_DIM)
    query_blocks = queries.reshape(span_count, SPAN, head_count, HEAD_DIM)
    scores = jnp.einsum(
        "cqhd,ckhd->chqk", query_blocks, key_blocks, preferred_element_type=jnp.float32
    )
    scores = scores / math.sqrt(HEAD_DIM)
    weights = jax.nn.softmax(scores, axis=-1).astype(jnp.bfloat16)
    attended = jnp.einsum(
        "chqk,ckhd->cqhd", weights, value_blocks, preferred_element_type=jnp.float32
    )
    attended = attended.astype(jnp.bfloat16).reshape(span_count * SPAN, inner_width)
    partial_terms = jnp.dot(
        attended,
        lax.all_gather(out_weight, "dp", axis=1, tiled=True),
        preferred_element_type=jnp.float32,
    )
    return lax.psum_scatter(
        partial_terms.astype(jnp.bfloat16), "mp", scatter_dimension=1, tiled=True
    )


def solution(mesh):
    in_specs = (
        P("dp", "mp"),
        P("dp", None),
        P(None, "mp"),
        P(None, "mp"),
        P("mp", "dp"),
        P("dp", None),
    )
    out_specs = P("dp", "mp")
    return jax.shard_map(
        on_device, mesh=mesh, in_specs=in_specs, out_specs=out_specs, check_vma=False
    )
```

profile of v0, /device:TPU:1, one launch (start us, length us, event | category | flops | bytes accessed | tf_op | source)
XLA Modules:
  0.0 459.4 jit_solution(4644224904882574688)
XLA Ops:
  6.5 0.0 copy-start
  6.5 0.8 reshape.185
  7.4 0.1 select_reduce_fusion
  7.5 0.1 copy.24
  7.6 23.1 %all_to_all.17 = s32[32,1,1]{2,1,0:T(1,128)S(1)} all-to-all(s32[32,1,1]{2,1,0:T(1,128)S(1)} %copy.24), channel_id=1, replica_groups=mesh['dp'=32,'mp'=16] {'dp'}, dimensions={0} | all-to-all | bytes 256 | tf_op jit(solution)/shard_map/all_to_all | solution.py:25
  30.6 0.7 reduce
  31.3 0.0 copy-done
  31.3 4.4 gather_fusion
  35.7 0.0 copy-start.4
  35.7 0.0 copy-start.1
  35.7 0.0 copy-start.2
  35.7 5.0 %all-to-all-start.1 = ((bf16[32,128,896]{2,1,0:T(8,128)(2,1)}), bf16[32,128,896]{2,1,0:T(8,128)(2,1)}, u32[]{:S(2)}, u32[]{:S(2)}) async-start(bf16[32,128,896]{2,1,0:T(8,128)(2,1)} %gather_fusion), calls=%async_computation.1 | async-start | bytes 14680064 | tf_op jit(solution)/shard_map/all_to_all | solution.py:28
  40.8 0.0 copy-start.3
  40.8 0.0 all-gather.2.cloned.1.call-start
  40.8 0.7 all-gather.2.cloned.1.call-update
  41.5 0.0 reduce-scatter.2.cloned.1.call-start
  41.6 0.0 copy-done.4
  41.6 0.1 reshape.186
  41.7 0.0 copy-done.1
  41.7 221.5 %all-to-all-done.1 = bf16[32,128,896]{2,1,0:T(8,128)(2,1)} async-done(((bf16[32,128,896]{2,1,0:T(8,128)(2,1)}), bf16[32,128,896]{2,1,0:T(8,128)(2,1)}, u32[]{:S(2)}, u32[]{:S(2)}) %all-to-all-start.1) | async-done | bytes 7340064 | tf_op jit(solution)/shard_map/all_to_all | solution.py:28
  263.3 3.8 gather_fusion.1
  267.1 0.0 copy-done.2
  267.1 0.4 convolution_convert_fusion.1
  267.6 0.1 reshape.189
  267.6 0.0 copy-done.3
  267.6 0.4 convolution_convert_fusion.2
  268.1 0.1 reshape.188
  268.1 0.2 fusion.2
  268.4 0.2 fusion.14
  268.6 0.5 fusion.4
  269.1 0.1 copy.28
  269.2 58.5 %all-gather.2.cloned.1.call-done = bf16[256,8192]{1,0:T(8,128)(2,1)} async-done(((bf16[256,256]{1,0:T(8,128)(2,1)}), bf16[256,8192]{1,0:T(8,128)(2,1)}) %all-gather.2.cloned.1.call-update) | async-done | bytes 4194320 | tf_op jit(solution)/shard_map/all_gather | solution.py:50
  327.7 4.3 convolution_convert_fusion
  331.9 0.0 reduce-scatter.2.cloned.1.call-update
  332.0 120.6 %reduce-scatter.2.cloned.1.call-done = bf16[128,512]{1,0:T(8,128)(2,1)} async-done(((bf16[128,8192]{1,0:T(8,128)(2,1)}), bf16[128,512]{1,0:T(8,128)(2,1)}) %reduce-scatter.2.cloned.1.call-update) | async-done | bytes 131088 | tf_op jit(solution)/shard_map/reduce_scatter | solution.py:53
  (6 shorter events, 0.1 us)
Async XLA Ops:
  6.5 24.8 %copy-start = (bf16[512,896]{1,0:T(8,128)(2,1)S(1)}, bf16[512,896]{1,0:T(8,128)(2,1)}, u32[]{:S(2)}) copy-start(bf16[512,896]{1,0:T(8,128)(2,1)} %param.7) | copy-start | bytes 2752516
  35.7 5.9 %copy-start.4 = (s32[2,2]{1,0:T(2,128)S(1)}, s32[2,2]{1,0:T(2,128)}, u32[]{:S(2)}) copy-start(s32[2,2]{1,0:T(2,128)} %param.11) | copy-start | bytes 52
  35.7 5.9 %copy-start.1 = (bf16[128,256]{1,0:T(8,128)(2,1)S(1)}, bf16[128,256]{1,0:T(8,128)(2,1)}, u32[]{:S(2)}) copy-start(bf16[128,256]{1,0:T(8,128)(2,1)} %param.6) | copy-start | bytes 196612
  35.7 231.4 %copy-start.2 = (bf16[896,256]{1,0:T(8,128)(2,1)S(1)}, bf16[896,256]{1,0:T(8,128)(2,1)}, u32[]{:S(2)}) copy-start(bf16[896,256]{1,0:T(8,128)(2,1)} %param.8) | copy-start | bytes 1376260
  35.7 227.5 %all-to-all-start.1 = ((bf16[32,128,896]{2,1,0:T(8,128)(2,1)}), bf16[32,128,896]{2,1,0:T(8,128)(2,1)}, u32[]{:S(2)}, u32[]{:S(2)}) async-start(bf16[32,128,896]{2,1,0:T(8,128)(2,1)} %gather_fusion), calls=%async_computation.1 | async-start | bytes 14680064 | tf_op jit(solution)/shard_map/all_to_all | solution.py:28
  40.8 226.8 %copy-start.3 = (bf16[896,256]{1,0:T(8,128)(2,1)S(1)}, bf16[896,256]{1,0:T(8,128)(2,1)}, u32[]{:S(2)}) copy-start(bf16[896,256]{1,0:T(8,128)(2,1)} %param.9) | copy-start | bytes 1376260
  40.8 286.9 %all-gather.2.cloned.1.call-start = ((), (), s32[]{:S(2)}) async-start(), calls=%async_computation.3 | async-start | bytes 4325376 | tf_op jit(solution)/shard_map/all_gather | solution.py:50
  41.5 411.1 %reduce-scatter.2.cloned.1.call-start = ((), (), s32[]{:S(2)}) async-start(), calls=%async_computation.4 | async-start | bytes 2228224 | tf_op jit(solution)/shard_map/reduce_scatter | solution.py:53
Sparse Core Ops, SparseCore 0:
  43.6 283.9 all-gather.1
  332.5 120.0 reduce-scatter.1
where the time goes:
time: 460 us; the launch traced here: 459 us
  waiting for transfers between devices  401 us (87%)
  blocking collectives  23.1 us (5%)
  between operations  13.5 us (3%)
  local copies, waits for them, and re-layouts  9.5 us (2%)
  matrix products  5.86 us (1%)
  starting transfers between devices  5.12 us (1%)
    all_to_all x1, waiting for transfers between devices, on_device(): lax.all_to_all(outgoing, 'dp', split_axis=0, concat_axis=0, tiled=True)  222 us
    reduce_scatter x1, waiting for transfers between devices, on_device(): lax.psum_scatter(partial_terms.astype(jnp.bfloat16), 'mp', scatter_dimens...  121 us
    all_gather x1, waiting for transfers between devices, on_device(): lax.all_gather(out_weight, 'dp', axis=1, tiled=True)  58.5 us
    all_to_all x1, blocking collectives, on_device(): lax.all_to_all(wanted, 'dp', split_axis=0, concat_axis=0, tiled=True)  23.1 us
  transfers between devices with their start and end apart: 3, of which 3 were waited for; matrix products, arithmetic and copies ran while one was open for 1% of the time, Pallas kernels for 0%

commit v1 on v0

--- a/solution.py
+++ b/solution.py
@@ -47,7 +47,9 @@
     attended = attended.astype(jnp.bfloat16).reshape(span_count * SPAN, inner_width)
     partial_terms = jnp.dot(
         attended,
-        lax.all_gather(out_weight, "dp", axis=1, tiled=True),
+        jnp.concatenate(
+            lax.all_to_all(jnp.stack([out_weight] * lax.axis_size("dp")), "dp", 0, 0), axis=1
+        ),
         preferred_element_type=jnp.float32,
     )
     return lax.psum_scatter(

time: 460 us -> 528 us (1.15)
  waiting for transfers between devices: 401 us -> 438 us
  starting transfers between devices: 5.12 us -> 33.9 us
    all_to_all x0 -> x1, waiting for transfers between devices: none -> 96.6 us  [on_device(): lax.all_to_all(jnp.stack([out_weight] * lax.axis_size('dp')), 'dp', 0, 0)]
    all_gather x1 -> x0, waiting for transfers between devices: 58.5 us -> none  [on_device(): lax.all_gather(out_weight, 'dp', axis=1, tiled=True)]
    all_to_all x0 -> x1, starting transfers between devices: none -> 28.8 us  [on_device(): lax.all_to_all(jnp.stack([out_weight] * lax.axis_size('dp')), 'dp', 0, 0)]
    all_to_all x1, waiting for transfers between devices: 222 us -> 200 us  [on_device(): lax.all_to_all(outgoing, 'dp', split_axis=0, concat_axis=0, tiled=True)]
    reduce_scatter x1, waiting for transfers between devices: 121 us -> 141 us  [on_device(): lax.psum_scatter(partial_terms.astype(jnp.bfloat16), 'mp', scatter_dimens...]
where the time goes in v1:
time: 528 us
  waiting for transfers between devices  438 us (83%)
  starting transfers between devices  33.9 us (6%)
  blocking collectives  23.1 us (4%)
  between operations  13.6 us (3%)
  local copies, waits for them, and re-layouts  12.1 us (2%)
  matrix products  6.62 us (1%)
    all_to_all x1, waiting for transfers between devices, on_device(): lax.all_to_all(outgoing, 'dp', split_axis=0, concat_axis=0, tiled=True)  200 us
    reduce_scatter x1, waiting for transfers between devices, on_device(): lax.psum_scatter(partial_terms.astype(jnp.bfloat16), 'mp', scatter_dimens...  141 us
    all_to_all x1, waiting for transfers between devices, on_device(): lax.all_to_all(jnp.stack([out_weight] * lax.axis_size('dp')), 'dp', 0, 0)  96.6 us
    all_to_all x1, starting transfers between devices, on_device(): lax.all_to_all(jnp.stack([out_weight] * lax.axis_size('dp')), 'dp', 0, 0)  28.8 us
    all_to_all x1, blocking collectives, on_device(): lax.all_to_all(wanted, 'dp', split_axis=0, concat_axis=0, tiled=True)  23.1 us
  transfers between devices with their start and end apart: 3, of which 3 were waited for; matrix products, arithmetic and copies ran while one was open for 1% of the time, Pallas kernels for 0%

profile of v1, /device:TPU:1, one launch (start us, length us, event | category | flops | bytes accessed | tf_op | source)
XLA Modules:
  0.0 527.9 jit_solution(14895714873590767199)
XLA Ops:
  6.5 0.0 copy-start
  6.5 0.8 reshape.193
  7.4 0.1 select_reduce_fusion
  7.5 0.1 copy.27
  7.6 23.1 %all_to_all.22 = s32[32,1,1]{2,1,0:T(1,128)S(1)} all-to-all(s32[32,1,1]{2,1,0:T(1,128)S(1)} %copy.27), channel_id=1, replica_groups=mesh['dp'=32,'mp'=16] {'dp'}, dimensions={0} | all-to-all | bytes 256 | tf_op jit(solution)/shard_map/all_to_all | solution.py:25
  30.6 0.7 reduce
  31.3 0.0 copy-done
  31.3 4.4 gather_fusion
  35.7 0.0 copy-start.1
  35.7 5.0 all-to-all-start.1
  40.8 0.0 copy-done.1
  40.8 0.1 copy.32
  40.9 200.3 %all-to-all-done.1 = bf16[32,128,896]{2,1,0:T(8,128)(2,1)} async-done(((bf16[32,128,896]{2,1,0:T(8,128)(2,1)}), bf16[32,128,896]{2,1,0:T(8,128)(2,1)}, u32[]{:S(2)}, u32[]{:S(2)}) %all-to-all-start.1) | async-done | bytes 7340064 | tf_op jit(solution)/shard_map/all_to_all | solution.py:28
  241.2 2.5 stack.2
  243.7 0.0 copy-start.5
  243.7 0.0 copy-start.2
  243.7 0.0 copy-start.3
  243.7 0.0 copy-start.4
  243.7 28.8 %all-to-all-start.2 = ((bf16[32,256,256]{1,2,0:T(8,128)(2,1)}), bf16[32,256,256]{1,2,0:T(8,128)(2,1)}, u32[]{:S(2)}, u32[]{:S(2)}) async-start(bf16[32,256,256]{1,2,0:T(8,128)(2,1)} %stack.2), calls=%async_computation.2 | async-start | bytes 8388608 | tf_op jit(solution)/shard_map/all_to_all | solution.py:51
  272.5 0.0 reduce-scatter.2.cloned.1.call-start
  272.6 0.0 copy-done.5
  272.6 0.1 reshape.194
  272.7 0.0 copy-done.2
  272.7 3.8 gather_fusion.1
  276.5 0.0 copy-done.3
  276.5 0.4 convolution_convert_fusion.1
  277.0 0.1 reshape.197
  277.1 0.0 copy-done.4
  277.1 0.4 convolution_convert_fusion.2
  277.5 0.1 reshape.196
  277.6 0.2 fusion.2
  277.8 0.2 fusion.14
  278.0 0.5 fusion.4
  278.5 0.1 copy.31
  278.6 96.6 %all-to-all-done.2 = bf16[32,256,256]{1,2,0:T(8,128)(2,1)} async-done(((bf16[32,256,256]{1,2,0:T(8,128)(2,1)}), bf16[32,256,256]{1,2,0:T(8,128)(2,1)}, u32[]{:S(2)}, u32[]{:S(2)}) %all-to-all-start.2) | async-done | bytes 4194336 | tf_op jit(solution)/shard_map/all_to_all | solution.py:51
  375.2 5.0 convolution_convert_fusion
  380.2 0.0 reduce-scatter.2.cloned.1.call-update
  380.3 140.8 %reduce-scatter.2.cloned.1.call-done = bf16[128,512]{1,0:T(8,128)(2,1)} async-done(((bf16[128,8192]{1,0:T(8,128)(2,1)}), bf16[128,512]{1,0:T(8,128)(2,1)}) %reduce-scatter.2.cloned.1.call-update) | async-done | bytes 131088 | tf_op jit(solution)/shard_map/reduce_scatter | solution.py:55
  (6 shorter events, 0.1 us)
Async XLA Ops:
  6.5 24.8 %copy-start = (bf16[512,896]{1,0:T(8,128)(2,1)S(1)}, bf16[512,896]{1,0:T(8,128)(2,1)}, u32[]{:S(2)}) copy-start(bf16[512,896]{1,0:T(8,128)(2,1)} %param.7) | copy-start | bytes 2752516
  35.7 5.1 copy-start.1
  35.7 205.5 %all-to-all-start.1 = ((bf16[32,128,896]{2,1,0:T(8,128)(2,1)}), bf16[32,128,896]{2,1,0:T(8,128)(2,1)}, u32[]{:S(2)}, u32[]{:S(2)}) async-start(bf16[32,128,896]{2,1,0:T(8,128)(2,1)} %gather_fusion), calls=%async_computation.1 | async-start | bytes 14680064 | tf_op jit(solution)/shard_map/all_to_all | solution.py:28
  243.7 28.9 %copy-start.5 = (s32[2,2]{1,0:T(2,128)S(1)}, s32[2,2]{1,0:T(2,128)}, u32[]{:S(2)}) copy-start(s32[2,2]{1,0:T(2,128)} %param.11) | copy-start | bytes 52
  243.7 29.0 %copy-start.2 = (bf16[128,256]{1,0:T(8,128)(2,1)S(1)}, bf16[128,256]{1,0:T(8,128)(2,1)}, u32[]{:S(2)}) copy-start(bf16[128,256]{1,0:T(8,128)(2,1)} %param.6) | copy-start | bytes 196612
  243.7 32.8 %copy-start.3 = (bf16[896,256]{1,0:T(8,128)(2,1)S(1)}, bf16[896,256]{1,0:T(8,128)(2,1)}, u32[]{:S(2)}) copy-start(bf16[896,256]{1,0:T(8,128)(2,1)} %param.8) | copy-start | bytes 1376260
  243.7 33.3 %copy-start.4 = (bf16[896,256]{1,0:T(8,128)(2,1)S(1)}, bf16[896,256]{1,0:T(8,128)(2,1)}, u32[]{:S(2)}) copy-start(bf16[896,256]{1,0:T(8,128)(2,1)} %param.9) | copy-start | bytes 1376260
  243.7 131.5 %all-to-all-start.2 = ((bf16[32,256,256]{1,2,0:T(8,128)(2,1)}), bf16[32,256,256]{1,2,0:T(8,128)(2,1)}, u32[]{:S(2)}, u32[]{:S(2)}) async-start(bf16[32,256,256]{1,2,0:T(8,128)(2,1)} %stack.2), calls=%async_computation.2 | async-start | bytes 8388608 | tf_op jit(solution)/shard_map/all_to_all | solution.py:51
  272.5 248.5 %reduce-scatter.2.cloned.1.call-start = ((), (), s32[]{:S(2)}) async-start(), calls=%async_computation.4 | async-start | bytes 2228224 | tf_op jit(solution)/shard_map/reduce_scatter | solution.py:55
Sparse Core Ops, SparseCore 0:
  380.4 140.6 reduce-scatter.1
